TPU v7x, 32 devices: a whole 2x2x4 slice. The times are simulated.
32 devices in a mesh: dp: 4 (over y, x), row: 2 (over core), col: 4 (over z).
Axes of the slice: x: 2, y: 2, z: 4, core: 2. Of those that a mesh axis runs over, the one named last changes fastest.
Arguments:
- inputs: bfloat16 [8192, 1536], P('dp', 'row'), may hold values from -6 to 6
- segments: int32 [4, 2048], P('dp'), may hold values from 0 to 5, never falling along the last dimension, each value on 1 to 1024 neighbouring positions
- cotangent: bfloat16 [8192, 1536], P('dp', 'row'), may hold values from -6 to 6
- norm_gain: float32 [1536], P('row'), may hold values from 0.1 to 1.9
- gate_proj: float32 [1536, 48, 64], P('dp', 'col', 'row'), may hold values from -0.15625 to 0.15625
- inner_proj: float32 [1536, 48, 64], P('dp', 'col', 'row'), may hold values from -0.15625 to 0.15625
- state_proj: float32 [1536, 256], P('dp'), may hold values from -0.15625 to 0.15625
- step_proj: float32 [1536, 48], P('dp', 'col'), may hold values from -0.15625 to 0.15625
- conv_inner: float32 [4, 48, 64], P(None, 'col', 'row'), may hold values from -0.5 to 0.5
- bias_inner: float32 [48, 64], P('col', 'row'), may hold values from -0.5 to 0.5
- conv_state: float32 [4, 256], replicated, may hold values from -0.5 to 0.5
- bias_state: float32 [256], replicated, may hold values from -0.5 to 0.5
- step_bias: float32 [48], P('col'), may hold values from -3 to -1
- decay_log: float32 [48], P('col'), may hold values from -2.3 to 1.4
- skip_gain: float32 [48], P('col'), may hold values from 0.25 to 1
- gate_norm: float32 [48, 64], P('col', 'row'), may hold values from 0.1 to 1.9
- out_proj: float32 [1536, 48, 64], P('dp', 'col', 'row'), may hold values from -0.109375 to 0.109375
Outputs:
- output: bfloat16 [8192, 1536], P('dp', 'row')
- grad_inputs: float32 [8192, 1536], P('dp', 'row')
- grad_norm_gain: float32 [1536], P('row')
- grad_gate_proj: float32 [1536, 48, 64], P('dp', 'col', 'row')
- grad_inner_proj: float32 [1536, 48, 64], P('dp', 'col', 'row')
- grad_state_proj: float32 [1536, 256], P('dp')
- grad_step_proj: float32 [1536, 48], P('dp', 'col')
- grad_conv_inner: float32 [4, 48, 64], P(None, 'col', 'row')
- grad_bias_inner: float32 [48, 64], P('col', 'row')
- grad_conv_state: float32 [4, 256], replicated
- grad_bias_state: float32 [256], replicated
- grad_step_bias: float32 [48], P('col')
- grad_decay_log: float32 [48], P('col')
- grad_skip_gain: float32 [48], P('col')
- grad_gate_norm: float32 [48, 64], P('col', 'row')
- grad_out_proj: float32 [1536, 48, 64], P('dp', 'col', 'row')
Inputs may be any that keep to these rules, and one draw needn't show every extreme that they name: `segments`: in each sequence the numbers never fall; a document is a run of equal numbers of at most 1024 tokens, and one document has exactly 1024.
All inputs are finite; a program needn't handle non-finite values.
Results may differ from a plain program's by a relative error of at most 0.012.
The roundings to bfloat16 on the way count: a program that leaves them out, or rounds other values in their place, can miss the bound.
Values may be sent and summed in bfloat16 or wider, within the bound.
A program may use at most 192 MiB of HBM per device.

v0:
```python
import jax
import jax.numpy as jnp
from jax import lax
from jax.sharding import PartitionSpec as P

H = 48
P_SIZE = 64
BLOCK_LEN = 256
EPSILON = 1e-05
HIGHEST = lax.Precision.HIGHEST


def conv_act(values, kernel, offset_bias, seg_ids):
    length = values.shape[0]
    width_k = kernel.shape[0]
    summed = offset_bias[None, :] + kernel[width_k - 1][None, :] * values
    for offset in range(1, width_k):
        shifted = jnp.pad(values, ((offset, 0), (0, 0)))[:length]
        earlier = jnp.pad(seg_ids, (offset, 0), constant_values=-1)[:length]
        within = (earlier == seg_ids).astype(jnp.float32)
        summed = summed + kernel[width_k - 1 - offset][None, :] * shifted * within[:, None]
    return jax.nn.silu(summed)


def ssm_gate(
    gate_pre, inner_act, state_act, step_size, decay_rate, skip_vals, seg_ids, head_count, block_len
):
    length = gate_pre.shape[0]
    channels = inner_act.shape[1] // head_count
    state_dim = state_act.shape[1] // 2
    block_count = length // block_len
    inner_heads = inner_act.reshape(length, head_count, channels)
    log_decay = step_size * decay_rate[None, :]
    cumul = jnp.cumsum(log_decay.reshape(block_count, block_len, head_count), axis=1)
    seg_blocks = seg_ids.reshape(block_count, block_len)
    driven = (inner_heads * step_size[:, :, None]).reshape(
        block_count, block_len, head_count, channels
    )
    in_blocks = state_act[:, :state_dim].reshape(block_count, block_len, state_dim)
    out_blocks = state_act[:, state_dim:].reshape(block_count, block_len, state_dim)
    positions = jnp.arange(block_len)
    causal = positions[:, None] >= positions[None, :]

    def intra_block(item):
        cum_block, seg_block, in_block, out_block, driven_block = item
        inner_prod = jnp.dot(out_block, in_block.T, precision=HIGHEST)
        gaps = cum_block.T[:, :, None] - cum_block.T[:, None, :]
        allowed = (causal & (seg_block[:, None] == seg_block[None, :]))[None]
        decays = jnp.where(allowed, jnp.exp(jnp.where(allowed, gaps, 0.0)), 0.0)
        mixing = decays * inner_prod[None]
        return jnp.einsum("hts,shp->thp", mixing, driven_block, precision=HIGHEST)

    local_out = lax.map(
        jax.checkpoint(intra_block), (cumul, seg_blocks, in_blocks, out_blocks, driven)
    )
    last_cum = cumul[:, -1, :]
    last_seg = seg_blocks[:, -1]
    tails = jnp.where(
        seg_blocks[:, :, None] == last_seg[:, None, None],
        jnp.exp(last_cum[:, None, :] - cumul),
        0.0,
    )
    contrib = jnp.einsum("kqhp,kqn->khpn", driven * tails[..., None], in_blocks, precision=HIGHEST)
    before_seg = jnp.concatenate([jnp.full((1,), -1, seg_ids.dtype), last_seg[:-1]])
    carried = (last_seg == before_seg).astype(jnp.float32)

    def advance(state, item):
        keep_flag, last_block, contrib_block = item
        renewed = keep_flag * jnp.exp(last_block)[:, None, None] * state + contrib_block
        return (renewed, state)

    initial = jnp.zeros((head_count, channels, state_dim), jnp.float32)
    final_state, entering = lax.scan(advance, initial, (carried, last_cum, contrib))
    reach = jnp.where(seg_blocks[:, :, None] == before_seg[:, None, None], jnp.exp(cumul), 0.0)
    from_state = (
        jnp.einsum("kqn,khpn->kqhp", out_blocks, entering, precision=HIGHEST) * reach[..., None]
    )
    mixed = (local_out + from_state).reshape(length, head_count, channels) + skip_vals[
        None, :, None
    ] * inner_heads
    gated = mixed * jax.nn.silu(gate_pre.reshape(length, head_count, channels))
    return gated.reshape(length, head_count * channels)


def contract_last(left, right):
    return lax.dot_general(
        left, right, (((1,), (1,)), ((), ())), preferred_element_type=jnp.float32
    )


def contract_first(left, right):
    return lax.dot_general(
        left, right, (((0,), (0,)), ((), ())), preferred_element_type=jnp.float32
    )


def per_device(
    inputs,
    segments,
    cotangent,
    norm_gain,
    gate_proj,
    inner_proj,
    state_proj,
    step_proj,
    conv_inner,
    bias_inner,
    conv_state,
    bias_state,
    step_bias,
    decay_log,
    skip_gain,
    gate_norm,
    out_proj,
):
    seg_ids = segments[0]
    length = inputs.shape[0]
    row_count = lax.axis_size("row")
    col_count = lax.axis_size("col")
    row_at = lax.axis_index("row")
    col_at = lax.axis_index("col")
    group_size = row_count * col_count
    model_width = inputs.shape[1] * row_count
    head_count = gate_proj.shape[1]
    channels = gate_proj.shape[2]
    local_width = head_count * channels
    state_width = state_proj.shape[1]
    pieces = model_width // group_size
    member = row_at * col_count + col_at
    state_share = state_width // group_size
    half_heads = head_count // row_count
    inner_width = H * P_SIZE
    plain = inputs.astype(jnp.float32)
    sq_total = lax.psum(jnp.sum(plain * plain, axis=1), "row")
    scaling = lax.rsqrt(sq_total / model_width + EPSILON)
    normed_half = (plain * scaling[:, None] * norm_gain[None, :]).astype(jnp.bfloat16)
    normed = lax.all_gather(normed_half, "row", axis=1, tiled=True)
    gathered = (
        lax.all_gather(gate_proj.astype(jnp.bfloat16), "dp", axis=0, tiled=True),
        lax.all_gather(inner_proj.astype(jnp.bfloat16), "dp", axis=0, tiled=True),
        lax.all_gather(state_proj.astype(jnp.bfloat16), "dp", axis=0, tiled=True),
        lax.all_gather(step_proj.astype(jnp.bfloat16), "dp", axis=0, tiled=True),
        lax.all_gather(out_proj.astype(jnp.bfloat16), "dp", axis=0, tiled=True),
    )
    gate_w = gathered[0].reshape(model_width, local_width)
    inner_w = gathered[1].reshape(model_width, local_width)
    state_w = gathered[2]
    step_w = gathered[3]
    out_w = gathered[4].reshape(model_width, local_width)
    gate_pre = jnp.dot(normed, gate_w, preferred_element_type=jnp.float32)
    inner_pre = jnp.dot(normed, inner_w, preferred_element_type=jnp.float32)
    state_pre = jnp.dot(normed, state_w, preferred_element_type=jnp.float32)
    step_pre = jnp.dot(normed, step_w, preferred_element_type=jnp.float32)
    step_arg = step_pre + step_bias[None, :]
    step_size = jax.nn.softplus(step_arg)
    decay_rate = -jnp.exp(decay_log)

    def state_conv(pre_vals, kernel, offset_bias):
        return conv_act(pre_vals, kernel, offset_bias, seg_ids)

    state_act, state_back = jax.vjp(state_conv, state_pre, conv_state, bias_state)

    def mixer(
        gate_vals, inner_vals, state_vals, step_vals, decay_vals, skip_vals, kernel, offset_bias
    ):
        inner_act = conv_act(inner_vals, kernel, offset_bias, seg_ids)
        return ssm_gate(
            gate_vals,
            inner_act,
            state_vals,
            step_vals,
            decay_vals,
            skip_vals,
            seg_ids,
            head_count,
            BLOCK_LEN,
        )

    gated, mixer_back = jax.vjp(
        mixer,
        gate_pre,
        inner_pre,
        state_act,
        step_size,
        decay_rate,
        skip_gain,
        conv_inner.reshape(conv_inner.shape[0], local_width),
        bias_inner.reshape(local_width),
    )
    gsum = lax.psum(jnp.sum(gated * gated, axis=1), ("row", "col"))
    gate_scale = lax.rsqrt(gsum / inner_width + EPSILON)
    gain_flat = gate_norm.reshape(local_width)
    normed_gate = (gated * gate_scale[:, None] * gain_flat[None, :]).astype(jnp.bfloat16)
    partial_out = contract_last(normed_gate, out_w)
    out_slice = lax.psum_scatter(partial_out, ("row", "col"), scatter_dimension=1, tiled=True)
    plain_slice = lax.dynamic_slice_in_dim(plain, col_at * pieces, pieces, 1)
    out_rows = (plain_slice + out_slice).astype(jnp.bfloat16)
    output = lax.all_gather(out_rows, "col", axis=1, tiled=True)
    cot_full = lax.all_gather(cotangent, "row", axis=1, tiled=True)
    d_normed_gate = jnp.dot(cot_full, out_w, preferred_element_type=jnp.float32)
    grad_out = contract_first(cot_full, normed_gate)
    grad_gate_gain = jnp.sum(d_normed_gate * gated * gate_scale[:, None], axis=0)
    weighted = d_normed_gate * gain_flat[None, :]
    gate_dot = lax.psum(jnp.sum(weighted * gated, axis=1), ("row", "col"))
    d_gated = (
        gate_scale[:, None] * weighted - gated * (gate_scale**3 * gate_dot / inner_width)[:, None]
    )
    d_gate_pre, d_inner_pre, d_state_act, d_step, d_decay, d_skip, d_conv_in, d_bias_in = (
        mixer_back(d_gated)
    )
    wide_heads = head_count * col_count
    wide_step = lax.dynamic_update_slice_in_dim(
        jnp.zeros((length, wide_heads), jnp.float32), d_step, col_at * head_count, 1
    )
    wide_decay = lax.dynamic_update_slice_in_dim(
        jnp.zeros((wide_heads,), jnp.float32), d_decay, col_at * head_count, 0
    )
    wide_skip = lax.dynamic_update_slice_in_dim(
        jnp.zeros((wide_heads,), jnp.float32), d_skip, col_at * head_count, 0
    )
    shared = lax.psum((d_state_act, wide_step, wide_decay, wide_skip), ("row", "col"))
    d_state_full = shared[0]
    d_step_full = lax.dynamic_slice_in_dim(shared[1], col_at * head_count, head_count, 1)
    d_decay_full = lax.dynamic_slice_in_dim(shared[2], col_at * head_count, head_count, 0)
    d_skip_full = lax.dynamic_slice_in_dim(shared[3], col_at * head_count, head_count, 0)
    d_state_pre, grad_conv_st, grad_bias_st = state_back(d_state_full)
    d_step_arg = d_step_full * jax.nn.sigmoid(step_arg)
    grad_step_bias = jnp.sum(d_step_arg, axis=0)
    grad_decay = d_decay_full * decay_rate
    gate_low = d_gate_pre.astype(jnp.bfloat16)
    inner_low = d_inner_pre.astype(jnp.bfloat16)
    state_low = d_state_pre.astype(jnp.bfloat16)
    step_low = d_step_arg.astype(jnp.bfloat16)
    state_part = contract_last(
        lax.dynamic_slice_in_dim(state_low, member * state_share, state_share, 1),
        lax.dynamic_slice_in_dim(state_w, member * state_share, state_share, 1),
    )
    step_part = contract_last(
        lax.dynamic_slice_in_dim(step_low, row_at * half_heads, half_heads, 1),
        lax.dynamic_slice_in_dim(step_w, row_at * half_heads, half_heads, 1),
    )
    d_normed = (
        contract_last(gate_low, gate_w) + contract_last(inner_low, inner_w) + state_part + step_part
    )
    grad_gate_w = contract_first(normed, gate_low)
    grad_inner_w = contract_first(normed, inner_low)
    grad_state_w = contract_first(normed, state_low)
    grad_step_w = contract_first(normed, step_low)
    cot_plain = cotangent.astype(jnp.float32)
    d_half = lax.psum_scatter(d_normed, "row", scatter_dimension=1, tiled=True)
    d_half = lax.psum(d_half, "col")
    weighted_in = d_half * norm_gain[None, :]
    input_dot = lax.psum(jnp.sum(weighted_in * plain, axis=1), "row")
    grad_rows = (
        cot_plain
        + scaling[:, None] * weighted_in
        - plain * (scaling**3 * input_dot / model_width)[:, None]
    )
    grad_norm = jnp.sum(d_half * plain * scaling[:, None], axis=0)
    big = (
        lax.psum_scatter(
            grad_gate_w.reshape(model_width, head_count, channels),
            "dp",
            scatter_dimension=0,
            tiled=True,
        ),
        lax.psum_scatter(
            grad_inner_w.reshape(model_width, head_count, channels),
            "dp",
            scatter_dimension=0,
            tiled=True,
        ),
        lax.psum_scatter(grad_state_w, "dp", scatter_dimension=0, tiled=True),
        lax.psum_scatter(grad_step_w, "dp", scatter_dimension=0, tiled=True),
        lax.psum_scatter(
            grad_out.reshape(model_width, head_count, channels),
            "dp",
            scatter_dimension=0,
            tiled=True,
        ),
    )
    small = lax.psum(
        (
            grad_norm,
            d_conv_in.reshape(conv_inner.shape),
            d_bias_in.reshape(bias_inner.shape),
            grad_conv_st,
            grad_bias_st,
            grad_step_bias,
            grad_decay,
            d_skip_full,
            grad_gate_gain.reshape(gate_norm.shape),
        ),
        "dp",
    )
    return (
        output,
        grad_rows,
        small[0],
        big[0],
        big[1],
        big[2],
        big[3],
        small[1],
        small[2],
        small[3],
        small[4],
        small[5],
        small[6],
        small[7],
        small[8],
        big[4],
    )


def solution(mesh):
    return jax.shard_map(
        per_device,
        mesh=mesh,
        in_specs=(
            P("dp", "row"),
            P("dp", None),
            P("dp", "row"),
            P("row"),
            P("dp", "col", "row"),
            P("dp", "col", "row"),
            P("dp", None),
            P("dp", "col"),
            P(None, "col", "row"),
            P("col", "row"),
            P(),
            P(),
            P("col"),
            P("col"),
            P("col"),
            P("col", "row"),
            P("dp", "col", "row"),
        ),
        out_specs=(
            P("dp", "row"),
            P("dp", "row"),
            P("row"),
            P("dp", "col", "row"),
            P("dp", "col", "row"),
            P("dp", None),
            P("dp", "col"),
            P(None, "col", "row"),
            P("col", "row"),
            P(),
            P(),
            P("col"),
            P("col"),
            P("col"),
            P("col", "row"),
            P("dp", "col", "row"),
        ),
        check_vma=False,
    )
```

profile of v0, /device:TPU:0, one launch (start us, length us, event | category | flops | bytes accessed | tf_op | source)
XLA Modules:
  0.0 1333.0 jit_solution(18420000439808059908)
XLA Ops:
  23.6 10.2 all_gather.26
  33.9 14.0 %all_gather.27 = bf16[1536,256]{1,0:T(8,128)(2,1)} all-gather(bf16[384,256]{1,0:T(8,128)(2,1)S(1)} %convert_element_type.83), channel_id=1, replica_groups=mesh['dp'=4,'row'=2,'col'=4] {'dp'}, dimensions={0}, use_global_device_ids=true | all-gather | bytes 983040 | tf_op jit(solution)/shard_map/all_gather | solution.py:141
  50.5 11.6 all-gather.7.cloned.1.call-done
  110.1 54.1 %while.72 = (s32[]{:T(128)}, f32[12,32,128]{2,1,0:T(8,128)S(1)}, f32[8,12,32,128]{3,2,1,0:T(8,128)}, f32[8,12]{1,0:T(8,128)}, f32[8,12,1,1]{1,3,2,0:T(1,128)}, /...) while((s32[]{:T(128)}, f32[12,32,128]{2,1,0:T(8,128)S(1)}, ...), condition=%wide.region_7.8_spmd.clone, body=%wide.region_6.7_spmd.clone.sunk | while | flops 196635 | bytes 985236 | solution.py:73
  172.3 57.1 %while.70 = (s32[]{:T(128)}, f32[8,256,12,32]{1,3,2,0:T(8,128)}, f32[8,256,12,32]{1,3,2,0:T(8,128)S(1)}, s32[8,256]{1,0:T(8,128)}, f32[8,256,12]{1,2,0:T(8,128)}...) while((s32[]{:T(128)}, f32[8,256,12,32]{1,3,2,0:T(8,128)}, ...), condition=%wide.region_5.6_spmd.clone, body=%wide.region_4.5_spmd.clone.sunk | while | flops 405995520 | bytes 1766501 | solution.py:53
  236.3 9.7 multiply_reduce_fusion.9
  246.0 17.5 %psum.127 = f32[2048]{0:T(1024)S(1)} all-reduce(f32[2048]{0:T(1024)S(1)} %get-tuple-element.940), channel_id=1, replica_groups=mesh['dp'=4,'row'=2,'col'=4] {'row','col'}, use_global_device_ids=true, to_apply=%region_9.10 | all-reduce | flops 2048 | bytes 16384 | tf_op jit(solution)/shard_map/psum | solution.py:190
  271.6 14.0 %psum.128 = f32[2048]{0:T(1024)S(1)} all-reduce(f32[2048]{0:T(1024)S(1)} %get-tuple-element.834), channel_id=1, replica_groups=mesh['dp'=4,'row'=2,'col'=4] {'row','col'}, use_global_device_ids=true, to_apply=%region_12.13 | all-reduce | flops 2048 | bytes 16384 | tf_op jit(solution)/shard_map/psum | solution.py:204
  304.5 114.0 %while.71 = (s32[]{:T(128)}, f32[8,256,12]{1,2,0:T(8,128)S(1)}, f32[8,256,128]{2,1,0:T(8,128)}, f32[8,256,128]{2,1,0:T(8,128)}, f32[8,256,12,32]{1,3,2,0:T(8,128...) while((s32[]{:T(128)}, f32[8,256,12]{1,2,0:T(8,128)S(1)}, ...), condition=%wide.region_20.21_spmd.clone, body=%wide.region_16.20_spmd.clone.sunk | while | flops 917897216 | bytes 6503601 | solution.py:53
  419.8 36.3 %while.73 = (s32[]{:T(128)}, f32[12,32,128]{2,1,0:T(8,128)S(1)}, f32[8,12]{1,0:T(8,128)S(1)}, f32[8,12,32,128]{3,2,1,0:T(8,128)}, f32[8,12,32,128]{3,2,1,0:T(8,1...) while((s32[]{:T(128)}, f32[12,32,128]{2,1,0:T(8,128)S(1)}, ...), condition=%wide.region_15.16_spmd.clone, body=%wide.region_13.15_spmd.clone.sunk | while | flops 294928 | bytes 1180264 | solution.py:73
  484.5 19.9 %reduce-window.16 = f32[8,12,2,128]{3,1,2,0:T(8,128)S(1)} reduce-window(f32[8,12,2,128]{3,1,2,0:T(8,128)S(1)} %copy.159, f32[]{:T(128)} %constant.213.clone.1), window={size=1x1x1x128 pad=0_0x0_0x0_0x0_127}, to_apply=%region_26.27 | reduce-window | flops 3121152 | bytes 196612 | tf_op jit(solution)/shard_map/reduce-window.2
  523.5 9.5 multiply_reduce_fusion.5
  548.2 31.2 %all-reduce.34.cloned.1.call-done = (f32[2048,256]{1,0:T(8,128)}, f32[2048,48]{0,1:T(8,128)}) async-done(((f32[2048,256]{1,0:T(8,128)}, f32[2048,48]{0,1:T(8,128)}), (f32[2048,256]{1,0:T(8,128)}, f32[2048,48]{0,1:T(8,128)})) %all-reduce.34.cloned.1.call-update) | async-done | bytes 2490384 | tf_op jit(solution)/shard_map/psum | solution.py:221
  593.6 17.8 %fusion.60 = f32[2048,1536]{1,0:T(8,128)} fusion(f32[2048,1536]{1,0:T(8,128)} %fusion.126, f32[2048,1536]{1,0:T(8,128)} %fusion.161, f32[2048,1536,1]{1,0,2:T(8,128)} %fusion.160, bf16[2048,12]{0,1:T(8,128)(2,1)S(1)} %get-tuple-element.937, s32[]{:T(128)S(6)} %select_n.96, bf16[1536,12]{0,1:T(8,128)(2,1)S(1)} %copy-done.50), kind=kOutput, calls=%fused_computation.77 | convolution fusion | flops 47185920 | bytes 50390016 | tf_op jit(solution)/shard_map/dot_general | solution.py:86
  616.5 210.1 %reduce-scatter.22.cloned.1.call-done = f32[192,2048]{1,0:T(8,128)} async-done(((f32[1536,2048]{1,0:T(8,128)}), f32[192,2048]{1,0:T(8,128)}) %reduce-scatter.22.cloned.1.call-update) | async-done | bytes 1572880
  835.9 15.8 %reduce-scatter.10.cloned.1.call-done = f32[2048,768]{1,0:T(8,128)} async-done(((f32[2048,1536]{1,0:T(8,128)}), f32[2048,768]{1,0:T(8,128)}) %reduce-scatter.10.cloned.1.call-update) | async-done | bytes 6291472 | tf_op jit(solution)/shard_map/reduce_scatter | solution.py:250
  885.5 18.0 %all-reduce.26 = (f32[48]{0:T(128)S(1)}, f32[48]{0:T(128)S(1)}) all-reduce(f32[48]{0:T(128)S(1)} %dynamic_update_slice.85, f32[48]{0:T(128)S(1)} %dynamic_update_slice.86), channel_id=1, replica_groups=mesh['dp'=4,'row'=2,'col'=4] {'row','col'}, use_global_device_ids=true, to_apply=%region_56.57 | all-reduce | flops 96 | bytes 768 | tf_op jit(solution)/shard_map/psum | solution.py:221
  903.7 15.4 %all-gather.15.cloned.1.call-done = bf16[2048,768]{0,1:T(8,128)(2,1)} async-done(((bf16[2048,192]{0,1:T(8,128)(2,1)}), bf16[2048,768]{0,1:T(8,128)(2,1)}) %all-gather.15.cloned.1.call-update) | async-done | bytes 3145744 | tf_op jit(solution)/shard_map/all_gather | solution.py:198
  923.6 219.5 %all-reduce.32.cloned.1.call-done = f32[2048,768]{1,0:T(8,128)} async-done(((f32[2048,768]{1,0:T(8,128)}), f32[2048,768]{1,0:T(8,128)}) %all-reduce.32.cloned.1.call-update) | async-done | bytes 6291472 | tf_op jit(solution)/shard_map/psum | solution.py:251
  1147.3 17.6 %all-reduce.28 = (f32[768]{0:T(1024)}, f32[4,12,32]{2,1,0:T(8,128)S(1)}, f32[12,32]{1,0:T(8,128)}, f32[4,256]{1,0:T(4,128)}, f32[256]{0:T(256)}, /*index=5*/f32[...) all-reduce(f32[768]{0:T(1024)S(1)} %get-tuple-element.831, ...), channel_id=1, replica_groups=mesh['dp'=4,'row'=2,'col'=4] {'dp'}, use_global_device_ids=true, to_apply=%region_34.35 | all-reduce | flops 4388 | bytes 35104 | tf_op jit(solution)/shard_map/psum | solution.py:282
  1174.2 29.1 %reduce-scatter.16.cloned.1.call-done = f32[384,256]{1,0:T(8,128)} async-done(((f32[1536,256]{1,0:T(8,128)}), f32[384,256]{1,0:T(8,128)}) %reduce-scatter.16.cloned.1.call-update) | async-done | bytes 393232 | tf_op jit(solution)/shard_map/reduce_scatter | solution.py:273
  1203.2 41.0 %reduce-scatter.12.cloned.1.call-done = f32[384,12,32]{0,2,1:T(8,128)} async-done(((f32[1536,12,32]{0,2,1:T(8,128)}), f32[384,12,32]{0,2,1:T(8,128)}) %reduce-scatter.12.cloned.1.call-update) | async-done | bytes 589840 | tf_op jit(solution)/shard_map/reduce_scatter | solution.py:261
  1244.3 40.9 %reduce-scatter.14.cloned.1.call-done = f32[384,12,32]{0,2,1:T(8,128)} async-done(((f32[1536,12,32]{0,2,1:T(8,128)}), f32[384,12,32]{0,2,1:T(8,128)}) %reduce-scatter.14.cloned.1.call-update) | async-done | bytes 589840 | tf_op jit(solution)/shard_map/reduce_scatter | solution.py:267
  1285.2 40.9 %reduce-scatter.20.cloned.1.call-done = f32[384,12,32]{0,2,1:T(8,128)} async-done(((f32[1536,12,32]{0,2,1:T(8,128)}), f32[384,12,32]{0,2,1:T(8,128)}) %reduce-scatter.20.cloned.1.call-update) | async-done | bytes 589840 | tf_op jit(solution)/shard_map/reduce_scatter | solution.py:275
  (621 shorter events, 512.4 us)
Async XLA Ops:
  7.2 43.3 %all-gather.9.cloned.1.call-start = ((), (), s32[]{:S(2)}) async-start(), calls=%async_computation.8 | async-start | bytes 1474560 | tf_op jit(solution)/shard_map/all_gather | solution.py:140
  9.2 52.9 %all-gather.7.cloned.1.call-start = ((), (), s32[]{:S(2)}) async-start(), calls=%async_computation.7 | async-start | bytes 9437184 | tf_op jit(solution)/shard_map/all_gather | solution.py:137
  17.7 218.7 %all-gather.11.cloned.1.call-start = ((), (), s32[]{:S(2)}) async-start(), calls=%async_computation.9 | async-start | bytes 1474560 | tf_op jit(solution)/shard_map/all_gather | solution.py:139
  19.4 244.1 %all-gather.13.cloned.1.call-start = ((), (), s32[]{:S(2)}) async-start(), calls=%async_computation.10 | async-start | bytes 1474560 | tf_op jit(solution)/shard_map/all_gather | solution.py:143
  20.2 243.3 %all-gather.17.cloned.1.call-start = ((), (), s32[]{:S(2)}) async-start(), calls=%async_computation.12 | async-start | bytes 9437184 | tf_op jit(solution)/shard_map/all_gather | solution.py:199
  20.8 558.6 %all-reduce.34.cloned.1.call-start = ((), (), s32[]{:S(2)}) async-start(), calls=%async_computation.21 | async-start | bytes 4980736 | tf_op jit(solution)/shard_map/psum | solution.py:221
  22.1 45.9 %copy-start.51 = (s32[8,256]{1,0:T(8,128)}, s32[8,256]{1,0:T(8,128)S(1)}, u32[]{:S(2)}) copy-start(s32[8,256]{1,0:T(8,128)S(1)} %reshape_squeeze.2) | copy-start | bytes 24580
  22.6 45.4 %copy-start.45 = (f32[2048]{0:T(1024)}, f32[2048]{0:T(1024)S(1)}, u32[]{:S(2)}) copy-start(f32[2048]{0:T(1024)S(1)} %get-tuple-element.976) | copy-start | bytes 24580
  22.7 45.3 %copy-start.70 = (f32[384]{0:T(512)}, f32[384]{0:T(512)S(1)}, u32[]{:S(2)}) copy-start(f32[384]{0:T(512)S(1)} %mul.739) | copy-start | bytes 4612
  22.8 45.2 %copy-start.72 = (f32[384]{0:T(512)}, f32[384]{0:T(512)S(1)}, u32[]{:S(2)}) copy-start(f32[384]{0:T(512)S(1)} %mul.734) | copy-start | bytes 4612
  172.3 57.2 %copy-start.28 = (f32[8,256,12]{1,2,0:T(8,128)S(1)}, f32[8,256,12]{1,2,0:T(8,128)}, u32[]{:S(2)}) copy-start(f32[8,256,12]{1,2,0:T(8,128)} %get-tuple-element.970) | copy-start | bytes 294916
  304.5 115.3 %copy-start.98 = (f32[8]{0:T(128)S(1)}, f32[8]{0:T(128)}, u32[]{:S(2)}) copy-start(f32[8]{0:T(128)} %get-tuple-element.1435) | copy-start | bytes 100
  511.2 315.3 %reduce-scatter.22.cloned.1.call-start = ((), (), s32[]{:S(2)}) async-start(), calls=%async_computation.20 | async-start | bytes 14155776
  519.1 332.6 %reduce-scatter.10.cloned.1.call-start = ((), (), s32[]{:S(2)}) async-start(), calls=%async_computation.13 | async-start | bytes 18874368 | tf_op jit(solution)/shard_map/reduce_scatter | solution.py:250
  611.4 307.6 %all-gather.15.cloned.1.call-start = ((), (), s32[]{:S(2)}) async-start(), calls=%async_computation.11 | async-start | bytes 3932160 | tf_op jit(solution)/shard_map/all_gather | solution.py:198
  835.9 307.2 %all-reduce.32.cloned.1.call-start = ((), (), s32[]{:S(2)}) async-start(), calls=%async_computation.14 | async-start | bytes 12582912 | tf_op jit(solution)/shard_map/psum | solution.py:251
  851.7 322.5 %reduce-scatter.18.cloned.1.call-start = ((), (), s32[]{:S(2)}) async-start(), calls=%async_computation.18 | async-start | bytes 122880 | tf_op jit(solution)/shard_map/reduce_scatter | solution.py:274
  856.1 347.1 %reduce-scatter.16.cloned.1.call-start = ((), (), s32[]{:S(2)}) async-start(), calls=%async_computation.17 | async-start | bytes 1966080 | tf_op jit(solution)/shard_map/reduce_scatter | solution.py:273
  862.3 382.0 %reduce-scatter.12.cloned.1.call-start = ((), (), s32[]{:S(2)}) async-start(), calls=%async_computation.15 | async-start | bytes 2949120 | tf_op jit(solution)/shard_map/reduce_scatter | solution.py:261
  870.0 415.2 %reduce-scatter.14.cloned.1.call-start = ((), (), s32[]{:S(2)}) async-start(), calls=%async_computation.16 | async-start | bytes 2949120 | tf_op jit(solution)/shard_map/reduce_scatter | solution.py:267
  877.3 448.8 %reduce-scatter.20.cloned.1.call-start = ((), (), s32[]{:S(2)}) async-start(), calls=%async_computation.19 | async-start | bytes 2949120 | tf_op jit(solution)/shard_map/reduce_scatter | solution.py:275
  903.6 239.5 %copy-start.53 = (f32[2048]{0:T(1024)S(1)}, f32[2048]{0:T(1024)}, u32[]{:S(2)}) copy-start(f32[2048]{0:T(1024)} %copy-done.52) | copy-start | bytes 24580
  903.7 239.5 %copy-start.62 = (f32[768]{0:T(1024)S(1)}, f32[768]{0:T(1024)}, u32[]{:S(2)}) copy-start(f32[768]{0:T(1024)} %param.28) | copy-start | bytes 9220
  923.6 244.3 %copy-start.58 = (f32[2048]{0:T(1024)S(1)}, f32[2048]{0:T(1024)}, u32[]{:S(2)}) copy-start(f32[2048]{0:T(1024)} %copy-done.57) | copy-start | bytes 24580
  (98 other events, 835.8 us)
Sparse Core Ops, SparseCore 0:
  10.4 32.6 all-gather.8
  45.3 16.8 all-gather.6
  64.5 28.7 all-gather.10
  95.5 27.5 all-gather.12
  124.5 16.7 all-gather.16
  511.4 68.0 all-reduce.33
  581.8 244.6 reduce-scatter.21
  829.0 22.6 reduce-scatter.9
  853.9 65.0 all-gather.14
  921.4 221.7 all-reduce.31
  1146.6 22.1 reduce-scatter.17
  1172.3 30.9 reduce-scatter.15
  1206.9 37.3 reduce-scatter.11
  1247.8 37.3 reduce-scatter.13
  1288.7 37.3 reduce-scatter.19
where the time goes:
time: 1350 us; the launch traced here: 1330 us
  waiting for transfers between devices  656 us (49%)
  matrix products  274 us (20%)
  other arithmetic  165 us (12%)
  local copies, waits for them, and re-layouts  124 us (9%)
  blocking collectives  96.5 us (7%)
  between operations  15.6 us (1%)
    psum x1, waiting for transfers between devices, per_device(): d_half = lax.psum(d_half, 'col')  219 us
    unnamed x16, waiting for transfers between devices  211 us
    dot_general x24, matrix products, intra_block(): return jnp.einsum('hts,shp->thp', mixing, driven_block, precision=HIGHEST)  95.9 us
    dot_general x5, matrix products, contract_last(): lax.dot_general(left, right, (((1,), (1,)), ((), ())), preferred_element_...  44.8 us
    reduce_scatter x1, waiting for transfers between devices, per_device(): lax.psum_scatter(grad_gate_w.reshape(model_width, head_count, channels),...  41 us
    reduce_scatter x1, waiting for transfers between devices, per_device(): lax.psum_scatter(grad_inner_w.reshape(model_width, head_count, channels),...  40.9 us
    reduce_scatter x1, waiting for transfers between devices, per_device(): lax.psum_scatter(grad_out.reshape(model_width, head_count, channels), 'dp...  40.9 us
    dot_general x5, matrix products, contract_first(): lax.dot_general(left, right, (((0,), (0,)), ((), ())), preferred_element_...  32.7 us
  transfers between devices with their start and end apart: 15, of which 10 were waited for; matrix products, arithmetic and copies ran while one was open for 24% of the time, Pallas kernels for 0%

commit v1 on v0

--- a/solution.py
+++ b/solution.py
@@ -218,7 +218,7 @@
     wide_skip = lax.dynamic_update_slice_in_dim(
         jnp.zeros((wide_heads,), jnp.float32), d_skip, col_at * head_count, 0
     )
-    shared = lax.psum((d_state_act, wide_step, wide_decay, wide_skip), ("row", "col"))
+    shared = lax.psum(lax.psum((d_state_act, wide_step, wide_decay, wide_skip), "col"), "row")
     d_state_full = shared[0]
     d_step_full = lax.dynamic_slice_in_dim(shared[1], col_at * head_count, head_count, 1)
     d_decay_full = lax.dynamic_slice_in_dim(shared[2], col_at * head_count, head_count, 0)

time: 1350 us -> 1400 us (1.037)
  waiting for transfers between devices: 656 us -> 718 us
    psum x1 -> x2, waiting for transfers between devices: 31.2 us -> 100 us  [the longest x1 100 us: per_device(): lax.psum((d_state_act, wide_step, wide_decay, wide_skip), 'col')]
    reduce_scatter x1, waiting for transfers between devices: 41 us -> 8.33 us  [per_device(): lax.psum_scatter(grad_gate_w.reshape(model_width, head_count, channels),...]
    reduce_scatter x1, waiting for transfers between devices: 0.01 us -> 26.6 us  [per_device(): lax.psum_scatter(grad_step_w, 'dp', scatter_dimension=0, tiled=True)]
    unnamed x16 -> x17, waiting for transfers between devices: 211 us -> 198 us
  transfers between devices with their start and end apart: 15 -> 16, of which waited for: 10 -> 11; matrix products, arithmetic and copies ran while one was open for 24% -> 23% of each run, Pallas kernels for 0% -> 0%
where the time goes in v1:
time: 1400 us; the launch traced here: 1390 us
  waiting for transfers between devices  718 us (51%)
  matrix products  274 us (20%)
  other arithmetic  164 us (12%)
  local copies, waits for them, and re-layouts  124 us (9%)
  blocking collectives  92.8 us (7%)
  between operations  15.6 us (1%)
    psum x1, waiting for transfers between devices, per_device(): d_half = lax.psum(d_half, 'col')  219 us
    unnamed x17, waiting for transfers between devices  198 us
    psum x1, waiting for transfers between devices, per_device(): lax.psum((d_state_act, wide_step, wide_decay, wide_skip), 'col')  100 us
    dot_general x24, matrix products, intra_block(): return jnp.einsum('hts,shp->thp', mixing, driven_block, precision=HIGHEST)  95.9 us
    dot_general x5, matrix products, contract_last(): lax.dot_general(left, right, (((1,), (1,)), ((), ())), preferred_element_...  45 us
    reduce_scatter x1, waiting for transfers between devices, per_device(): lax.psum_scatter(grad_inner_w.reshape(model_width, head_count, channels),...  41.3 us
    reduce_scatter x1, waiting for transfers between devices, per_device(): lax.psum_scatter(grad_out.reshape(model_width, head_count, channels), 'dp...  41.2 us
    reduce_scatter x1, waiting for transfers between devices, per_device(): lax.psum_scatter(grad_state_w, 'dp', scatter_dimension=0, tiled=True)  34.4 us
  transfers between devices with their start and end apart: 16, of which 11 were waited for; matrix products, arithmetic and copies ran while one was open for 23% of the time, Pallas kernels for 0%

profile of v1, /device:TPU:0, one launch (start us, length us, event | category | flops | bytes accessed | tf_op | source)
XLA Modules:
  0.0 1390.8 jit_solution(13683185534554640422)
XLA Ops:
  23.6 10.3 all_gather.26
  33.9 14.0 %all_gather.27 = bf16[1536,256]{1,0:T(8,128)(2,1)} all-gather(bf16[384,256]{1,0:T(8,128)(2,1)S(1)} %convert_element_type.83), channel_id=1, replica_groups=mesh['dp'=4,'row'=2,'col'=4] {'dp'}, dimensions={0}, use_global_device_ids=true | all-gather | bytes 983040 | tf_op jit(solution)/shard_map/all_gather | solution.py:141
  50.4 11.7 all-gather.7.cloned.1.call-done
  110.1 53.9 %while.72 = (s32[]{:T(128)}, f32[12,32,128]{2,1,0:T(8,128)S(1)}, f32[8,12,32,128]{3,2,1,0:T(8,128)}, f32[8,12]{1,0:T(8,128)}, f32[8,12,1,1]{1,3,2,0:T(1,128)}, /...) while((s32[]{:T(128)}, f32[12,32,128]{2,1,0:T(8,128)S(1)}, ...), condition=%wide.region_7.8_spmd.clone, body=%wide.region_6.7_spmd.clone.sunk | while | flops 196635 | bytes 985236 | solution.py:73
  172.1 57.1 %while.70 = (s32[]{:T(128)}, f32[8,256,12,32]{1,3,2,0:T(8,128)}, f32[8,256,12,32]{1,3,2,0:T(8,128)S(1)}, s32[8,256]{1,0:T(8,128)}, f32[8,256,12]{1,2,0:T(8,128)}...) while((s32[]{:T(128)}, f32[8,256,12,32]{1,3,2,0:T(8,128)}, ...), condition=%wide.region_5.6_spmd.clone, body=%wide.region_4.5_spmd.clone.sunk | while | flops 405995520 | bytes 1766501 | solution.py:53
  236.2 9.7 multiply_reduce_fusion.9
  245.8 17.5 %psum.155 = f32[2048]{0:T(1024)S(1)} all-reduce(f32[2048]{0:T(1024)S(1)} %get-tuple-element.945), channel_id=1, replica_groups=mesh['dp'=4,'row'=2,'col'=4] {'row','col'}, use_global_device_ids=true, to_apply=%region_9.10 | all-reduce | flops 2048 | bytes 16384 | tf_op jit(solution)/shard_map/psum | solution.py:190
  271.5 14.0 %psum.156 = f32[2048]{0:T(1024)S(1)} all-reduce(f32[2048]{0:T(1024)S(1)} %get-tuple-element.834), channel_id=1, replica_groups=mesh['dp'=4,'row'=2,'col'=4] {'row','col'}, use_global_device_ids=true, to_apply=%region_12.13 | all-reduce | flops 2048 | bytes 16384 | tf_op jit(solution)/shard_map/psum | solution.py:204
  304.4 114.0 %while.71 = (s32[]{:T(128)}, f32[8,256,12]{1,2,0:T(8,128)S(1)}, f32[8,256,128]{2,1,0:T(8,128)}, f32[8,256,128]{2,1,0:T(8,128)}, f32[8,256,12,32]{1,3,2,0:T(8,128...) while((s32[]{:T(128)}, f32[8,256,12]{1,2,0:T(8,128)S(1)}, ...), condition=%wide.region_20.21_spmd.clone, body=%wide.region_16.20_spmd.clone.sunk | while | flops 917897216 | bytes 6503601 | solution.py:53
  419.7 36.3 %while.73 = (s32[]{:T(128)}, f32[12,32,128]{2,1,0:T(8,128)S(1)}, f32[8,12]{1,0:T(8,128)S(1)}, f32[8,12,32,128]{3,2,1,0:T(8,128)}, f32[8,12,32,128]{3,2,1,0:T(8,1...) while((s32[]{:T(128)}, f32[12,32,128]{2,1,0:T(8,128)S(1)}, ...), condition=%wide.region_15.16_spmd.clone, body=%wide.region_13.15_spmd.clone.sunk | while | flops 294928 | bytes 1180264 | solution.py:73
  484.6 19.9 %reduce-window.16 = f32[8,12,2,128]{3,1,2,0:T(8,128)S(1)} reduce-window(f32[8,12,2,128]{3,1,2,0:T(8,128)S(1)} %copy.159, f32[]{:T(128)} %constant.213.clone.1), window={size=1x1x1x128 pad=0_0x0_0x0_0x0_127}, to_apply=%region_27.28 | reduce-window | flops 3121152 | bytes 196612 | tf_op jit(solution)/shard_map/reduce-window.2
  509.8 100.3 %all-reduce.37.cloned.1.call-done = (f32[2048,256]{1,0:T(8,128)}, f32[2048,48]{0,1:T(8,128)}) async-done(((f32[2048,256]{1,0:T(8,128)}, f32[2048,48]{0,1:T(8,128)}), (f32[2048,256]{1,0:T(8,128)}, f32[2048,48]{0,1:T(8,128)})) %all-reduce.37.cloned.1.call-update) | async-done | bytes 2490384 | tf_op jit(solution)/shard_map/psum | solution.py:221
  622.6 10.3 multiply_reduce_fusion.5
  662.1 17.9 %fusion.60 = f32[2048,1536]{1,0:T(8,128)} fusion(f32[2048,1536]{1,0:T(8,128)} %fusion.126, f32[2048,1536]{1,0:T(8,128)} %fusion.161, f32[2048,1536,1]{1,0,2:T(8,128)} %fusion.160, bf16[2048,12]{0,1:T(8,128)(2,1)S(1)} %get-tuple-element.942, s32[]{:T(128)S(6)} %select_n.96, bf16[1536,12]{0,1:T(8,128)(2,1)S(1)} %copy-done.52), kind=kOutput, calls=%fused_computation.77 | convolution fusion | flops 47185920 | bytes 50390016 | tf_op jit(solution)/shard_map/dot_general | solution.py:86
  685.0 197.7 %reduce-scatter.22.cloned.1.call-done = f32[192,2048]{1,0:T(8,128)} async-done(((f32[1536,2048]{1,0:T(8,128)}), f32[192,2048]{1,0:T(8,128)}) %reduce-scatter.22.cloned.1.call-update) | async-done | bytes 1572880
  892.1 15.8 %reduce-scatter.10.cloned.1.call-done = f32[2048,768]{1,0:T(8,128)} async-done(((f32[2048,1536]{1,0:T(8,128)}), f32[2048,768]{1,0:T(8,128)}) %reduce-scatter.10.cloned.1.call-update) | async-done | bytes 6291472 | tf_op jit(solution)/shard_map/reduce_scatter | solution.py:250
  941.5 12.3 all-reduce.26
  953.8 21.0 %all-gather.15.cloned.1.call-done = bf16[2048,768]{0,1:T(8,128)(2,1)} async-done(((bf16[2048,192]{0,1:T(8,128)(2,1)}), bf16[2048,768]{0,1:T(8,128)(2,1)}) %all-gather.15.cloned.1.call-update) | async-done | bytes 3145744 | tf_op jit(solution)/shard_map/all_gather | solution.py:198
  979.5 219.4 %all-reduce.35.cloned.1.call-done = f32[2048,768]{1,0:T(8,128)} async-done(((f32[2048,768]{1,0:T(8,128)}), f32[2048,768]{1,0:T(8,128)}) %all-reduce.35.cloned.1.call-update) | async-done | bytes 6291472 | tf_op jit(solution)/shard_map/psum | solution.py:251
  1205.7 19.5 %all-reduce.28 = (f32[768]{0:T(1024)}, f32[4,12,32]{2,1,0:T(8,128)S(1)}, f32[12,32]{1,0:T(8,128)}, f32[4,256]{1,0:T(4,128)}, f32[256]{0:T(256)}, /*index=5*/f32[...) all-reduce(f32[768]{0:T(1024)S(1)} %get-tuple-element.831, ...), channel_id=1, replica_groups=mesh['dp'=4,'row'=2,'col'=4] {'dp'}, use_global_device_ids=true, to_apply=%region_36.37 | all-reduce | flops 4388 | bytes 35104 | tf_op jit(solution)/shard_map/psum | solution.py:282
  1240.4 41.3 %reduce-scatter.14.cloned.1.call-done = f32[384,12,32]{0,2,1:T(8,128)} async-done(((f32[1536,12,32]{0,2,1:T(8,128)}), f32[384,12,32]{0,2,1:T(8,128)}) %reduce-scatter.14.cloned.1.call-update) | async-done | bytes 589840 | tf_op jit(solution)/shard_map/reduce_scatter | solution.py:267
  1281.7 41.2 %reduce-scatter.20.cloned.1.call-done = f32[384,12,32]{0,2,1:T(8,128)} async-done(((f32[1536,12,32]{0,2,1:T(8,128)}), f32[384,12,32]{0,2,1:T(8,128)}) %reduce-scatter.20.cloned.1.call-update) | async-done | bytes 589840 | tf_op jit(solution)/shard_map/reduce_scatter | solution.py:275
  1322.9 26.6 %reduce-scatter.18.cloned.1.call-done = f32[384,12]{0,1:T(8,128)} async-done(((f32[1536,12]{0,1:T(8,128)}), f32[384,12]{0,1:T(8,128)}) %reduce-scatter.18.cloned.1.call-update) | async-done | bytes 18448 | tf_op jit(solution)/shard_map/reduce_scatter | solution.py:274
  1349.5 34.4 %reduce-scatter.16.cloned.1.call-done = f32[384,256]{1,0:T(8,128)} async-done(((f32[1536,256]{1,0:T(8,128)}), f32[384,256]{1,0:T(8,128)}) %reduce-scatter.16.cloned.1.call-update) | async-done | bytes 393232 | tf_op jit(solution)/shard_map/reduce_scatter | solution.py:273
  (628 shorter events, 519.2 us)
Async XLA Ops:
  7.2 43.2 %all-gather.9.cloned.1.call-start = ((), (), s32[]{:S(2)}) async-start(), calls=%async_computation.8 | async-start | bytes 1474560 | tf_op jit(solution)/shard_map/all_gather | solution.py:140
  9.2 52.9 %all-gather.7.cloned.1.call-start = ((), (), s32[]{:S(2)}) async-start(), calls=%async_computation.7 | async-start | bytes 9437184 | tf_op jit(solution)/shard_map/all_gather | solution.py:137
  17.7 218.5 %all-gather.11.cloned.1.call-start = ((), (), s32[]{:S(2)}) async-start(), calls=%async_computation.9 | async-start | bytes 1474560 | tf_op jit(solution)/shard_map/all_gather | solution.py:139
  19.4 244.0 %all-gather.13.cloned.1.call-start = ((), (), s32[]{:S(2)}) async-start(), calls=%async_computation.10 | async-start | bytes 1474560 | tf_op jit(solution)/shard_map/all_gather | solution.py:143
  20.2 243.1 %all-gather.17.cloned.1.call-start = ((), (), s32[]{:S(2)}) async-start(), calls=%async_computation.12 | async-start | bytes 9437184 | tf_op jit(solution)/shard_map/all_gather | solution.py:199
  20.8 589.2 %all-reduce.37.cloned.1.call-start = ((), (), s32[]{:S(2)}) async-start(), calls=%async_computation.21 | async-start | bytes 4980736 | tf_op jit(solution)/shard_map/psum | solution.py:221
  22.1 45.9 %copy-start.53 = (s32[8,256]{1,0:T(8,128)}, s32[8,256]{1,0:T(8,128)S(1)}, u32[]{:S(2)}) copy-start(s32[8,256]{1,0:T(8,128)S(1)} %reshape_squeeze.2) | copy-start | bytes 24580
  172.1 57.2 %copy-start.30 = (f32[8,256,12]{1,2,0:T(8,128)S(1)}, f32[8,256,12]{1,2,0:T(8,128)}, u32[]{:S(2)}) copy-start(f32[8,256,12]{1,2,0:T(8,128)} %get-tuple-element.975) | copy-start | bytes 294916
  304.4 115.3 %copy-start.100 = (f32[8]{0:T(128)S(1)}, f32[8]{0:T(128)}, u32[]{:S(2)}) copy-start(f32[8]{0:T(128)} %get-tuple-element.1450) | copy-start | bytes 100
  506.6 103.6 %copy-start.12 = (f32[2048,12,32]{0,2,1:T(8,128)S(1)}, f32[2048,12,32]{0,2,1:T(8,128)}, u32[]{:S(2)}) copy-start(f32[2048,12,32]{0,2,1:T(8,128)} %copy-done.11) | copy-start | bytes 9437188
  509.7 138.3 %all-reduce.39.cloned.1.call-start = ((), (), s32[]{:S(2)}) async-start(), calls=%async_computation.22 | async-start | bytes 4980736 | tf_op jit(solution)/shard_map/psum | solution.py:221
  610.1 272.6 %reduce-scatter.22.cloned.1.call-start = ((), (), s32[]{:S(2)}) async-start(), calls=%async_computation.20 | async-start | bytes 14155776
  618.2 289.7 %reduce-scatter.10.cloned.1.call-start = ((), (), s32[]{:S(2)}) async-start(), calls=%async_computation.13 | async-start | bytes 18874368 | tf_op jit(solution)/shard_map/reduce_scatter | solution.py:250
  679.9 294.9 %all-gather.15.cloned.1.call-start = ((), (), s32[]{:S(2)}) async-start(), calls=%async_computation.11 | async-start | bytes 3932160 | tf_op jit(solution)/shard_map/all_gather | solution.py:198
  892.0 306.9 %all-reduce.35.cloned.1.call-start = ((), (), s32[]{:S(2)}) async-start(), calls=%async_computation.14 | async-start | bytes 12582912 | tf_op jit(solution)/shard_map/psum | solution.py:251
  907.9 332.5 %reduce-scatter.12.cloned.1.call-start = ((), (), s32[]{:S(2)}) async-start(), calls=%async_computation.15 | async-start | bytes 2949120 | tf_op jit(solution)/shard_map/reduce_scatter | solution.py:261
  915.2 366.5 %reduce-scatter.14.cloned.1.call-start = ((), (), s32[]{:S(2)}) async-start(), calls=%async_computation.16 | async-start | bytes 2949120 | tf_op jit(solution)/shard_map/reduce_scatter | solution.py:267
  922.8 400.1 %reduce-scatter.20.cloned.1.call-start = ((), (), s32[]{:S(2)}) async-start(), calls=%async_computation.19 | async-start | bytes 2949120 | tf_op jit(solution)/shard_map/reduce_scatter | solution.py:275
  930.2 419.3 %reduce-scatter.18.cloned.1.call-start = ((), (), s32[]{:S(2)}) async-start(), calls=%async_computation.18 | async-start | bytes 122880 | tf_op jit(solution)/shard_map/reduce_scatter | solution.py:274
  934.6 449.2 %reduce-scatter.16.cloned.1.call-start = ((), (), s32[]{:S(2)}) async-start(), calls=%async_computation.17 | async-start | bytes 1966080 | tf_op jit(solution)/shard_map/reduce_scatter | solution.py:273
  953.8 245.1 %copy-start.55 = (f32[2048]{0:T(1024)S(1)}, f32[2048]{0:T(1024)}, u32[]{:S(2)}) copy-start(f32[2048]{0:T(1024)} %copy-done.54) | copy-start | bytes 24580
  953.8 245.1 %copy-start.64 = (f32[768]{0:T(1024)S(1)}, f32[768]{0:T(1024)}, u32[]{:S(2)}) copy-start(f32[768]{0:T(1024)} %param.28) | copy-start | bytes 9220
  979.5 226.2 %copy-start.99 = (f32[12]{0:T(128)S(1)}, f32[12]{0:T(128)}, u32[]{:S(2)}) copy-start(f32[12]{0:T(128)} %param.38) | copy-start | bytes 148
  979.5 246.3 %copy-start.60 = (f32[2048]{0:T(1024)S(1)}, f32[2048]{0:T(1024)}, u32[]{:S(2)}) copy-start(f32[2048]{0:T(1024)} %copy-done.59) | copy-start | bytes 24580
  (101 other events, 886.4 us)
Sparse Core Ops, SparseCore 0:
  10.4 32.6 all-gather.8
  45.3 16.8 all-gather.6
  64.5 28.7 all-gather.10
  95.5 27.5 all-gather.12
  124.5 16.7 all-gather.16
  509.9 100.1 all-reduce.36
  612.5 21.0 all-reduce.38
  635.9 246.7 reduce-scatter.21
  885.1 22.7 reduce-scatter.9
  909.9 64.8 all-gather.14
  977.3 221.4 all-reduce.34
  1202.7 37.6 reduce-scatter.11
  1244.3 37.3 reduce-scatter.13
  1285.5 37.3 reduce-scatter.19
  1326.3 23.1 reduce-scatter.17
  1352.9 30.8 reduce-scatter.15
